TPU v7x, 256 devices: a whole 4x4x8 slice. The times are simulated.
256 devices in a mesh: leaf: 32 (over z, x), gx: 2 (over core), gy: 4 (over y).
Axes of the slice: x: 4, y: 4, z: 8, core: 2. Of those that a mesh axis runs over, the one named last changes fastest.
Arguments:
- leaf_rhs: float32 [32, 2, 4, 48, 16, 128], P('leaf', 'gx', 'gy'), may hold values from -6 to 6
- leaf_inv: float32 [32, 2, 4, 48, 128, 128], P('leaf', 'gx', 'gy'), may hold values from -0.4 to 1.7
- edge_blocks: float32 [32, 2, 4, 48, 2, 128, 128], P('leaf', 'gx', 'gy'), may hold values from -0.09375 to 0.09375
- edge_target: int32 [32, 2, 4, 48, 2], P('leaf', 'gx', 'gy'), may hold values from 0 to 639
- sep_rhs: float32 [32, 2, 4, 4, 16, 128], P('leaf', 'gx', 'gy'), may hold values from -6 to 6
- sep_inv: float32 [32, 2, 4, 4, 128, 128], P('leaf', 'gx', 'gy'), may hold values from -0.4 to 1.7
- sep_up: float32 [32, 2, 4, 4, 128, 128], P('leaf', 'gx', 'gy'), may hold values from -0.4375 to 0.4375
- sep_parent: int32 [32, 2, 4, 4], P('leaf', 'gx', 'gy'), may hold values from 0 to 3
Outputs:
- leaf_solution: float32 [32, 2, 4, 48, 16, 128], P('leaf', 'gx', 'gy')
- sep_solution: float32 [32, 2, 4, 4, 16, 128], P('leaf', 'gx', 'gy')
All inputs are finite; a program needn't handle non-finite values.
Results may differ from a plain program's by a relative error of at most 0.0003.
Values sent between devices are 32-bit elements; how exact they have to be, the bound alone decides.
No kernel may reach another device: no remote copies, remote signals or barrier semaphores. Data moves between devices by JAX's collectives and lax.ppermute only.
A program may use at most 64 MiB of HBM per device.

v0:
```python
import jax
import jax.numpy as jnp
from jax import lax
from jax.sharding import PartitionSpec as P

HIGHEST = lax.Precision.HIGHEST


def from_behind(value, axis, steps):
    count = lax.axis_size(axis)
    initial, last = (max(0, -steps), min(count, count - steps))
    return lax.ppermute(value, axis, [(source, source + steps) for source in range(initial, last)])


def extended(block, sides, width):
    for axis, dim in sides:
        count = lax.axis_size(axis)
        forward = [(i, i + 1) for i in range(count - 1)]
        backward = [(target, source) for source, target in forward]
        low = lax.ppermute(
            lax.slice_in_dim(block, block.shape[dim] - width, None, axis=dim), axis, forward
        )
        high = lax.ppermute(lax.slice_in_dim(block, 0, width, axis=dim), axis, backward)
        block = jnp.concatenate([low, block, high], axis=dim)
    return block


def along_rows(value, offset):
    return from_behind(value, "gx", offset)


def along_cols(value, offset):
    return from_behind(value, "gy", offset)


def along_levels(value, offset):
    return from_behind(value, "leaf", offset)


def local(leaf_rhs, leaf_inv, edge_blocks, edge_target, sep_rhs, sep_inv, sep_up, sep_parent):
    levels = lax.axis_size("leaf")
    rhs_leaf = leaf_rhs[0, 0, 0]
    inv_leaf = leaf_inv[0, 0, 0]
    blocks = edge_blocks[0, 0, 0]
    target = edge_target[0, 0, 0]
    rhs_sep = sep_rhs[0, 0, 0]
    inv_sep = sep_inv[0, 0, 0]
    up_blocks = sep_up[0, 0, 0]
    parent = sep_parent[0, 0, 0]
    slot_count, rhs_cols, block_width = rhs_leaf.shape
    sep_count = rhs_sep.shape[0]
    targets = 5 * levels * sep_count
    leaf_mid = jnp.einsum("srw,svw->srv", rhs_leaf, inv_leaf, precision=HIGHEST)
    products = jnp.einsum("srw,skvw->skrv", leaf_mid, blocks, precision=HIGHEST)
    chosen = (target[:, :, None] == jnp.arange(targets, dtype=jnp.int32)).astype(jnp.float32)
    outgoing = jnp.einsum("skt,skrv->trv", chosen, products, precision=HIGHEST)
    outgoing = outgoing.reshape(5, levels, sep_count, rhs_cols, block_width)
    arriving = outgoing[0] + along_rows(outgoing[2], 1) + along_rows(outgoing[1], -1)
    arriving = arriving + along_cols(outgoing[4], 1) + along_cols(outgoing[3], -1)
    updates = lax.psum_scatter(arriving, "leaf", scatter_dimension=0, tiled=True)[0]
    reduced = rhs_sep - updates
    parent_pick = (parent[:, None] == jnp.arange(sep_count, dtype=jnp.int32)).astype(jnp.float32)

    def solve_up(incoming):
        partial_mid = jnp.einsum("srw,svw->srv", reduced - incoming, inv_sep, precision=HIGHEST)
        lifted = jnp.einsum("crw,cvw->crv", partial_mid, up_blocks, precision=HIGHEST)
        return (partial_mid, jnp.einsum("cp,crv->prv", parent_pick, lifted, precision=HIGHEST))

    def solve_down(sep_mid, from_above):
        parents = jnp.einsum("cp,prw->crw", parent_pick, from_above, precision=HIGHEST)
        pushed = jnp.einsum("crv,cvw->crw", parents, up_blocks, precision=HIGHEST)
        return jnp.einsum("srv,svw->srw", sep_mid - pushed, inv_sep, precision=HIGHEST)

    empty = jnp.zeros_like(rhs_sep)

    def forward_step(turn, incoming):
        return along_levels(solve_up(incoming)[1], 1)

    incoming = lax.fori_loop(0, levels - 1, forward_step, empty)
    sep_mid = solve_up(incoming)[0]

    def backward_step(turn, from_above):
        return along_levels(solve_down(sep_mid, from_above), -1)

    from_above = lax.fori_loop(0, levels - 1, backward_step, empty)
    sep_sol = solve_down(sep_mid, from_above)
    every_level = lax.all_gather(sep_sol[None], "leaf", axis=0, tiled=True)
    padded = extended(every_level[None, None], (("gx", 0), ("gy", 1)), 1)
    solved_table = jnp.stack([padded[1, 1], padded[0, 1], padded[2, 1], padded[1, 0], padded[1, 2]])
    solved_table = solved_table.reshape(targets, rhs_cols * block_width)
    reached = jnp.dot(chosen.reshape(-1, targets), solved_table, precision=HIGHEST)
    reached = reached.reshape(slot_count, -1, rhs_cols, block_width)
    pulled_back = jnp.einsum("skrv,skvw->srw", reached, blocks, precision=HIGHEST)
    leaf_sol = jnp.einsum("srv,svw->srw", leaf_mid - pulled_back, inv_leaf, precision=HIGHEST)
    return (leaf_sol[None, None, None], sep_sol[None, None, None])


def solution(mesh):
    in_specs = (
        P("leaf", "gx", "gy", None, None, None),
        P("leaf", "gx", "gy", None, None, None),
        P("leaf", "gx", "gy", None, None, None, None),
        P("leaf", "gx", "gy", None, None),
        P("leaf", "gx", "gy", None, None, None),
        P("leaf", "gx", "gy", None, None, None),
        P("leaf", "gx", "gy", None, None, None),
        P("leaf", "gx", "gy", None),
    )
    out_specs = (P("leaf", "gx", "gy", None, None, None), P("leaf", "gx", "gy", None, None, None))
    return jax.shard_map(local, mesh=mesh, in_specs=in_specs, out_specs=out_specs, check_vma=False)
```

profile of v0, /device:TPU:1, one launch (start us, length us, event | category | flops | bytes accessed | tf_op | source)
XLA Modules:
  0.0 1161.4 jit_solution(9223311347620786621)
XLA Ops:
  15.0 7.4 fusion.24
  40.8 10.1 collective-permute-done.5
  54.5 219.2 %reduce-scatter.2.cloned.1.call-done = f32[1,4,16,128]{3,2,1,0:T(8,128)} async-done(((f32[32,4,16,128]{3,2,1,0:T(8,128)}), f32[1,4,16,128]{3,2,1,0:T(8,128)}) %reduce-scatter.2.cloned.1.call-update) | async-done | bytes 32784 | tf_op jit(solution)/shard_map/reduce_scatter | solution.py:60
  274.6 267.6 %while.22 = (s32[]{:T(128)}, f32[4,16,128]{2,0,1:T(4,128)S(1)}, f32[4,16,128]{2,0,1:T(4,128)S(1)}, f32[4,128,128]{2,1,0:T(8,128)S(1)}, f32[4,128,128]{2,1,0:T(8,128)}, /*index=5*/s32[4]{0:T(128)S(1)}, s32[]{:T(128)}) while((s32[]{:T(128)}, f32[4,16,128]{2,0,1:T(4,128)S(1)}, f32[4,16,128]{2,0,1:T(4,128)S(1)}, ...), condition=%wide.region_2.0_spmd.clone, body=%wide.region_1.0_spmd.clone.sunk | while | flops 25567264 | bytes 950405 | solution.py:79
  408.9 6.1 collective-permute-start
  490.2 6.1 collective-permute-start
  542.6 296.4 %while.23 = (s32[]{:T(128)}, f32[4,16,128]{2,1,0:T(8,128)S(1)}, f32[4,128,128]{2,1,0:T(8,128)}, f32[4,16,128]{2,1,0:T(8,128)S(1)}, f32[4,128,128]{2,1,0:T(8,128)S(1)}, /*index=5*/s32[4]{0:T(128)S(1)}, s32[]{:T(128)}) while((s32[]{:T(128)}, f32[4,16,128]{2,1,0:T(8,128)S(1)}, f32[4,128,128]{2,1,0:T(8,128)}, ...), condition=%wide.region_4.0_spmd.clone, body=%wide.region_3.0_spmd.clone.sunk | while | flops 25567264 | bytes 884869 | solution.py:85
  572.8 6.1 collective-permute-done.1
  634.3 6.1 collective-permute-done.1
  643.5 7.0 collective-permute-done.1
  653.6 6.8 collective-permute-done.1
  663.6 7.4 collective-permute-done.1
  674.2 6.7 collective-permute-done.1
  684.0 7.3 collective-permute-done.1
  694.5 6.9 collective-permute-done.1
  704.5 6.4 collective-permute-done.1
  714.1 6.3 collective-permute-done.1
  723.6 6.5 collective-permute-done.1
  733.2 7.2 collective-permute-done.1
  743.6 6.1 collective-permute-done.1
  752.9 6.8 collective-permute-done.1
  762.9 7.1 collective-permute-done.1
  773.2 6.4 collective-permute-done.1
  782.8 7.0 collective-permute-done.1
  793.0 6.8 collective-permute-done.1
  802.9 6.3 collective-permute-done.1
  812.4 6.7 collective-permute-done.1
  822.3 7.2 collective-permute-done.1
  832.7 6.4 collective-permute-done.1
  841.5 200.2 %all-gather.3.cloned.1.call-done = f32[128,16,128]{2,1,0:T(8,128)} async-done(((f32[4,16,128]{2,1,0:T(8,128)}), f32[128,16,128]{2,1,0:T(8,128)}) %all-gather.3.cloned.1.call-update) | async-done | bytes 1048592 | tf_op jit(solution)/shard_map/all_gather | solution.py:87
  1043.2 7.8 collective-permute-start.7
  1059.8 65.3 %collective-permute-done.8 = f32[3,1,32,4,16,128]{5,4,3,2,1,0:T(8,128)S(1)} collective-permute-done((f32[3,1,32,4,16,128]{5,4,3,2,1,0:T(8,128)S(1)}, f32[3,1,32,4,16,128]{5,4,3,2,1,0:T(8,128)S(1)}, u32[]{:S(2)}, u32[]{:S(2)}) %collective-permute-start.8) | collective-permute-done | bytes 3145760 | tf_op jit(solution)/shard_map/ppermute | solution.py:20
  (377 shorter events, 476.0 us)
Async XLA Ops:
  7.2 266.6 %reduce-scatter.2.cloned.1.call-start = ((), (), s32[]{:S(2)}) async-start(), calls=%async_computation.1 | async-start | bytes 1081344 | tf_op jit(solution)/shard_map/reduce_scatter | solution.py:60
  26.2 24.7 %collective-permute-start.5 = (f32[32,4,16,128]{3,2,1,0:T(8,128)S(1)}, f32[32,4,16,128]{3,2,1,0:T(8,128)S(1)}, u32[]{:S(2)}, u32[]{:S(2)}) collective-permute-start(f32[32,4,16,128]{3,2,1,0:T(8,128)S(1)} %copy.53), channel_id=1, source_target_pairs={{1,0},{2,1},{3,2},{5,4},{6,5},{7,6},{9,8},{10,9},{11,10},{13,12},{... | collective-permute-start | bytes 3145736 | tf_op jit(solution)/shard_map/ppermute | solution.py:12
  28.2 24.3 %collective-permute-start.4 = (f32[32,4,16,128]{3,2,1,0:T(8,128)S(1)}, f32[32,4,16,128]{3,2,1,0:T(8,128)S(1)}, u32[]{:S(2)}, u32[]{:S(2)}) collective-permute-start(f32[32,4,16,128]{3,2,1,0:T(8,128)S(1)} %copy.52), channel_id=1, source_target_pairs={{0,1},{1,2},{2,3},{4,5},{5,6},{6,7},{8,9},{9,10},{10,11},{12,13},{... | collective-permute-start | bytes 3145736 | tf_op jit(solution)/shard_map/ppermute | solution.py:12
  33.5 19.0 %collective-permute-start.3 = (f32[32,4,16,128]{3,2,1,0:T(8,128)S(1)}, f32[32,4,16,128]{3,2,1,0:T(8,128)S(1)}, u32[]{:S(2)}, u32[]{:S(2)}) collective-permute-start(f32[32,4,16,128]{3,2,1,0:T(8,128)S(1)} %copy.51), channel_id=1, source_target_pairs={{4,0},{5,1},{6,2},{7,3},{12,8},{13,9},{14,10},{15,11},{20,16},{21,... | collective-permute-start | bytes 3145736 | tf_op jit(solution)/shard_map/ppermute | solution.py:12
  39.4 13.1 %collective-permute-start.2 = (f32[32,4,16,128]{3,2,1,0:T(8,128)S(1)}, f32[32,4,16,128]{3,2,1,0:T(8,128)S(1)}, u32[]{:S(2)}, u32[]{:S(2)}) collective-permute-start(f32[32,4,16,128]{3,2,1,0:T(8,128)S(1)} %copy.49), channel_id=1, source_target_pairs={{0,4},{1,5},{2,6},{3,7},{8,12},{9,13},{10,14},{11,15},{16,20},{17,... | collective-permute-start | bytes 3145736 | tf_op jit(solution)/shard_map/ppermute | solution.py:12
  54.5 987.3 %all-gather.3.cloned.1.call-start = ((), (), s32[]{:S(2)}) async-start(), calls=%async_computation.2 | async-start | bytes 1081344 | tf_op jit(solution)/shard_map/all_gather | solution.py:87
  571.5 7.4 collective-permute-start.1
  633.0 7.4 collective-permute-start.1
  642.2 8.3 collective-permute-start.1
  652.3 8.1 collective-permute-start.1
  662.3 8.7 collective-permute-start.1
  672.9 8.0 collective-permute-start.1
  682.7 8.6 collective-permute-start.1
  693.2 8.2 collective-permute-start.1
  703.2 7.7 collective-permute-start.1
  712.8 7.6 collective-permute-start.1
  722.3 7.8 collective-permute-start.1
  731.9 8.5 collective-permute-start.1
  742.3 7.4 collective-permute-start.1
  751.6 8.1 collective-permute-start.1
  761.6 8.4 collective-permute-start.1
  771.9 7.7 collective-permute-start.1
  781.5 8.3 collective-permute-start.1
  791.7 8.1 collective-permute-start.1
  801.6 7.6 collective-permute-start.1
  811.1 8.0 collective-permute-start.1
  821.0 8.5 collective-permute-start.1
  831.4 7.7 collective-permute-start.1
  1041.8 9.5 collective-permute-start.6
  1043.2 10.2 collective-permute-start.7
  1055.0 70.2 %collective-permute-start.8 = (f32[3,1,32,4,16,128]{5,4,3,2,1,0:T(8,128)S(1)}, f32[3,1,32,4,16,128]{5,4,3,2,1,0:T(8,128)S(1)}, u32[]{:S(2)}, u32[]{:S(2)}) collective-permute-start(f32[3,1,32,4,16,128]{5,4,3,2,1,0:T(8,128)S(1)} %pad_maximum_fusion), channel_id=1, source_target_pairs={{0,1},{1,2},{2,3},{4,5},{5,6},{6,7},{8,9},{9,10},{10,11},{12,13},{... | collective-permute-start | bytes 9437192 | tf_op jit(solution)/shard_map/ppermute | solution.py:20
  1058.3 70.9 %collective-permute-start.9 = (f32[3,1,32,4,16,128]{5,4,3,2,1,0:T(8,128)S(1)}, f32[3,1,32,4,16,128]{5,4,3,2,1,0:T(8,128)S(1)}, u32[]{:S(2)}, u32[]{:S(2)}) collective-permute-start(f32[3,1,32,4,16,128]{5,4,3,2,1,0:T(8,128)S(1)} %pad_maximum_fusion), channel_id=1, source_target_pairs={{1,0},{2,1},{3,2},{5,4},{6,5},{7,6},{9,8},{10,9},{11,10},{13,12},{... | collective-permute-start | bytes 9437192 | tf_op jit(solution)/shard_map/ppermute | solution.py:23
  (48 other events, 1031.8 us)
Sparse Core Ops, SparseCore 0:
  54.6 219.0 reduce-scatter.1
  841.7 200.0 all-gather.2
where the time goes:
time: 1170 us; the launch traced here: 1160 us
  waiting for transfers between devices  732 us (63%)
  starting transfers between devices  234 us (20%)
  matrix products  159 us (14%)
  local copies, waits for them, and re-layouts  16.1 us (1%)
  between operations  14.3 us (1%)
    ppermute x66, waiting for transfers between devices, from_behind(): lax.ppermute(value, axis, [(source, source + steps) for source in range(i...  241 us
    ppermute x66, starting transfers between devices, from_behind(): lax.ppermute(value, axis, [(source, source + steps) for source in range(i...  220 us
    reduce_scatter x1, waiting for transfers between devices, local(): lax.psum_scatter(arriving, 'leaf', scatter_dimension=0, tiled=True)[0]  219 us
    all_gather x1, waiting for transfers between devices, local(): every_level = lax.all_gather(sep_sol[None], 'leaf', axis=0, tiled=True)  200 us
    ppermute x2, waiting for transfers between devices, extended(): lax.ppermute(lax.slice_in_dim(block, block.shape[dim] - width, None, axis...  65.6 us
    dot_general x31, matrix products, solve_up(): jnp.einsum('crw,cvw->crv', partial_mid, up_blocks, precision=HIGHEST)  45.6 us
    dot_general x32, matrix products, solve_down(): pushed = jnp.einsum('crv,cvw->crw', parents, up_blocks, precision=HIGHEST)  40.8 us
  transfers between devices with their start and end apart: 72, of which 70 were waited for; matrix products, arithmetic and copies ran while one was open for 0% of the time, Pallas kernels for 0%

commit v1 on v0

--- a/solution.py
+++ b/solution.py
@@ -84,7 +84,9 @@
 
     from_above = lax.fori_loop(0, levels - 1, backward_step, empty)
     sep_sol = solve_down(sep_mid, from_above)
-    every_level = lax.all_gather(sep_sol[None], "leaf", axis=0, tiled=True)
+    every_level = jnp.concatenate(
+        lax.all_to_all(jnp.stack([sep_sol[None]] * lax.axis_size("leaf")), "leaf", 0, 0), axis=0
+    )
     padded = extended(every_level[None, None], (("gx", 0), ("gy", 1)), 1)
     solved_table = jnp.stack([padded[1, 1], padded[0, 1], padded[2, 1], padded[1, 0], padded[1, 2]])
     solved_table = solved_table.reshape(targets, rhs_cols * block_width)

time: 1170 us -> 1120 us (0.957)
  waiting for transfers between devices: 732 us -> 532 us
  blocking collectives: 0 us -> 78.4 us
  starting transfers between devices: 234 us -> 307 us
    all_gather x1 -> x0, waiting for transfers between devices: 200 us -> none  [local(): every_level = lax.all_gather(sep_sol[None], 'leaf', axis=0, tiled=True)]
    all_to_all x0 -> x1, blocking collectives: none -> 78.4 us  [local(): lax.all_to_all(jnp.stack([sep_sol[None]] * lax.axis_size('leaf')), 'leaf'...]
    ppermute x2, starting transfers between devices: 9.05 us -> 82.2 us  [extended(): lax.ppermute(lax.slice_in_dim(block, 0, width, axis=dim), axis, backward)]
  transfers between devices with their start and end apart: 72 -> 71, of which waited for: 70 -> 69; matrix products, arithmetic and copies ran while one was open for 0% -> 0% of each run, Pallas kernels for 0% -> 0%
where the time goes in v1:
time: 1120 us; the launch traced here: 1110 us
  waiting for transfers between devices  532 us (48%)
  starting transfers between devices  307 us (27%)
  matrix products  158 us (14%)
  blocking collectives  78.4 us (7%)
  local copies, waits for them, and re-layouts  16.2 us (1%)
  between operations  14.3 us (1%)
    ppermute x66, waiting for transfers between devices, from_behind(): lax.ppermute(value, axis, [(source, source + steps) for source in range(i...  241 us
    ppermute x66, starting transfers between devices, from_behind(): lax.ppermute(value, axis, [(source, source + steps) for source in range(i...  220 us
    reduce_scatter x1, waiting for transfers between devices, local(): lax.psum_scatter(arriving, 'leaf', scatter_dimension=0, tiled=True)[0]  219 us
    ppermute x2, starting transfers between devices, extended(): lax.ppermute(lax.slice_in_dim(block, 0, width, axis=dim), axis, backward)  82.2 us
    all_to_all x1, blocking collectives, local(): lax.all_to_all(jnp.stack([sep_sol[None]] * lax.axis_size('leaf')), 'leaf'...  78.4 us
    ppermute x2, waiting for transfers between devices, extended(): lax.ppermute(lax.slice_in_dim(block, block.shape[dim] - width, None, axis...  65.4 us
    dot_general x31, matrix products, solve_up(): jnp.einsum('crw,cvw->crv', partial_mid, up_blocks, precision=HIGHEST)  45.6 us
    dot_general x32, matrix products, solve_down(): pushed = jnp.einsum('crv,cvw->crw', parents, up_blocks, precision=HIGHEST)  40.8 us
  transfers between devices with their start and end apart: 71, of which 69 were waited for; matrix products, arithmetic and copies ran while one was open for 0% of the time, Pallas kernels for 0%

profile of v1, /device:TPU:1, one launch (start us, length us, event | category | flops | bytes accessed | tf_op | source)
XLA Modules:
  0.0 1110.7 jit_solution(15617150365513127179)
XLA Ops:
  15.0 7.4 fusion.24
  40.8 10.1 collective-permute-done.5
  54.5 219.3 %reduce-scatter.2.cloned.1.call-done = f32[1,4,16,128]{3,2,1,0:T(8,128)} async-done(((f32[32,4,16,128]{3,2,1,0:T(8,128)}), f32[1,4,16,128]{3,2,1,0:T(8,128)}) %reduce-scatter.2.cloned.1.call-update) | async-done | bytes 32784 | tf_op jit(solution)/shard_map/reduce_scatter | solution.py:60
  274.6 267.6 %while.22 = (s32[]{:T(128)}, f32[4,16,128]{2,0,1:T(4,128)S(1)}, f32[4,16,128]{2,0,1:T(4,128)S(1)}, f32[4,128,128]{2,1,0:T(8,128)S(1)}, f32[4,128,128]{2,1,0:T(8,128)}, /*index=5*/s32[4]{0:T(128)S(1)}, s32[]{:T(128)}) while((s32[]{:T(128)}, f32[4,16,128]{2,0,1:T(4,128)S(1)}, f32[4,16,128]{2,0,1:T(4,128)S(1)}, ...), condition=%wide.region_2.0_spmd.clone, body=%wide.region_1.0_spmd.clone.sunk | while | flops 25567264 | bytes 950405 | solution.py:79
  408.9 6.1 collective-permute-start
  490.2 6.1 collective-permute-start
  542.6 296.4 %while.23 = (s32[]{:T(128)}, f32[4,16,128]{2,1,0:T(8,128)S(1)}, f32[4,128,128]{2,1,0:T(8,128)}, f32[4,16,128]{2,1,0:T(8,128)S(1)}, f32[4,128,128]{2,1,0:T(8,128)S(1)}, /*index=5*/s32[4]{0:T(128)S(1)}, s32[]{:T(128)}) while((s32[]{:T(128)}, f32[4,16,128]{2,1,0:T(8,128)S(1)}, f32[4,128,128]{2,1,0:T(8,128)}, ...), condition=%wide.region_4.0_spmd.clone, body=%wide.region_3.0_spmd.clone.sunk | while | flops 25567264 | bytes 884869 | solution.py:85
  572.8 6.1 collective-permute-done.1
  643.2 7.3 collective-permute-done.1
  653.7 6.7 collective-permute-done.1
  663.6 7.4 collective-permute-done.1
  674.2 6.7 collective-permute-done.1
  684.0 7.3 collective-permute-done.1
  694.5 6.4 collective-permute-done.1
  704.0 6.9 collective-permute-done.1
  714.1 6.3 collective-permute-done.1
  723.6 6.5 collective-permute-done.1
  733.2 7.2 collective-permute-done.1
  743.6 6.1 collective-permute-done.1
  752.9 6.9 collective-permute-done.1
  762.9 7.1 collective-permute-done.1
  773.2 6.4 collective-permute-done.1
  782.7 7.0 collective-permute-done.1
  792.9 6.8 collective-permute-done.1
  803.0 6.3 collective-permute-done.1
  812.4 6.7 collective-permute-done.1
  822.2 7.2 collective-permute-done.1
  832.6 6.4 collective-permute-done.1
  841.0 78.4 %all_to_all.5 = f32[32,1,4,16,128]{4,3,2,1,0:T(8,128)S(1)} all-to-all(f32[32,1,4,16,128]{4,3,2,1,0:T(8,128)S(1)} %stack.6), channel_id=1, replica_groups=mesh['leaf'=32,'gx'=2,'gy'=4] {'leaf'}, dimensions={0} | all-to-all | bytes 2097152 | tf_op jit(solution)/shard_map/all_to_all | solution.py:88
  920.7 80.9 %collective-permute-start.7 = (f32[1,1,32,4,16,128]{5,4,3,2,1,0:T(8,128)S(1)}, f32[1,1,32,4,16,128]{5,4,3,2,1,0:T(8,128)S(1)}, u32[]{:S(2)}, u32[]{:S(2)}) collective-permute-start(f32[1,1,32,4,16,128]{5,4,3,2,1,0:T(8,128)S(1)} %bitcast.139), channel_id=1, source_target_pairs={{4,0},{5,1},{6,2},{7,3},{12,8},{13,9},{14,10},{15,11},{20,16},{21,... | collective-permute-start | bytes 3145736 | tf_op jit(solution)/shard_map/ppermute | solution.py:23
  1009.1 65.3 %collective-permute-done.8 = f32[3,1,32,4,16,128]{5,4,3,2,1,0:T(8,128)S(1)} collective-permute-done((f32[3,1,32,4,16,128]{5,4,3,2,1,0:T(8,128)S(1)}, f32[3,1,32,4,16,128]{5,4,3,2,1,0:T(8,128)S(1)}, u32[]{:S(2)}, u32[]{:S(2)}) %collective-permute-start.8) | collective-permute-done | bytes 3145760 | tf_op jit(solution)/shard_map/ppermute | solution.py:20
  1083.3 6.0 copy.80
  (376 shorter events, 473.6 us)
Async XLA Ops:
  7.2 266.6 %reduce-scatter.2.cloned.1.call-start = ((), (), s32[]{:S(2)}) async-start(), calls=%async_computation.2 | async-start | bytes 1081344 | tf_op jit(solution)/shard_map/reduce_scatter | solution.py:60
  26.2 24.7 %collective-permute-start.5 = (f32[32,4,16,128]{3,2,1,0:T(8,128)S(1)}, f32[32,4,16,128]{3,2,1,0:T(8,128)S(1)}, u32[]{:S(2)}, u32[]{:S(2)}) collective-permute-start(f32[32,4,16,128]{3,2,1,0:T(8,128)S(1)} %copy.74), channel_id=1, source_target_pairs={{1,0},{2,1},{3,2},{5,4},{6,5},{7,6},{9,8},{10,9},{11,10},{13,12},{... | collective-permute-start | bytes 3145736 | tf_op jit(solution)/shard_map/ppermute | solution.py:12
  28.2 24.3 %collective-permute-start.4 = (f32[32,4,16,128]{3,2,1,0:T(8,128)S(1)}, f32[32,4,16,128]{3,2,1,0:T(8,128)S(1)}, u32[]{:S(2)}, u32[]{:S(2)}) collective-permute-start(f32[32,4,16,128]{3,2,1,0:T(8,128)S(1)} %copy.73), channel_id=1, source_target_pairs={{0,1},{1,2},{2,3},{4,5},{5,6},{6,7},{8,9},{9,10},{10,11},{12,13},{... | collective-permute-start | bytes 3145736 | tf_op jit(solution)/shard_map/ppermute | solution.py:12
  33.5 19.0 %collective-permute-start.3 = (f32[32,4,16,128]{3,2,1,0:T(8,128)S(1)}, f32[32,4,16,128]{3,2,1,0:T(8,128)S(1)}, u32[]{:S(2)}, u32[]{:S(2)}) collective-permute-start(f32[32,4,16,128]{3,2,1,0:T(8,128)S(1)} %copy.72), channel_id=1, source_target_pairs={{4,0},{5,1},{6,2},{7,3},{12,8},{13,9},{14,10},{15,11},{20,16},{21,... | collective-permute-start | bytes 3145736 | tf_op jit(solution)/shard_map/ppermute | solution.py:12
  39.4 13.1 %collective-permute-start.2 = (f32[32,4,16,128]{3,2,1,0:T(8,128)S(1)}, f32[32,4,16,128]{3,2,1,0:T(8,128)S(1)}, u32[]{:S(2)}, u32[]{:S(2)}) collective-permute-start(f32[32,4,16,128]{3,2,1,0:T(8,128)S(1)} %copy.70), channel_id=1, source_target_pairs={{0,4},{1,5},{2,6},{3,7},{8,12},{9,13},{10,14},{11,15},{16,20},{17,... | collective-permute-start | bytes 3145736 | tf_op jit(solution)/shard_map/ppermute | solution.py:12
  562.4 7.2 collective-permute-start.1
  571.5 7.4 collective-permute-start.1
  623.9 7.2 collective-permute-start.1
  641.9 8.6 collective-permute-start.1
  652.4 8.0 collective-permute-start.1
  662.3 8.7 collective-permute-start.1
  672.9 8.0 collective-permute-start.1
  682.7 8.6 collective-permute-start.1
  693.2 7.7 collective-permute-start.1
  702.7 8.2 collective-permute-start.1
  712.8 7.6 collective-permute-start.1
  722.3 7.8 collective-permute-start.1
  731.9 8.5 collective-permute-start.1
  742.3 7.4 collective-permute-start.1
  751.6 8.2 collective-permute-start.1
  761.6 8.4 collective-permute-start.1
  771.9 7.7 collective-permute-start.1
  781.4 8.3 collective-permute-start.1
  791.6 8.1 collective-permute-start.1
  801.7 7.6 collective-permute-start.1
  811.1 8.0 collective-permute-start.1
  820.9 8.5 collective-permute-start.1
  831.3 7.7 collective-permute-start.1
  919.4 82.3 %collective-permute-start.6 = (f32[1,1,32,4,16,128]{5,4,3,2,1,0:T(8,128)S(1)}, f32[1,1,32,4,16,128]{5,4,3,2,1,0:T(8,128)S(1)}, u32[]{:S(2)}, u32[]{:S(2)}) collective-permute-start(f32[1,1,32,4,16,128]{5,4,3,2,1,0:T(8,128)S(1)} %bitcast.138), channel_id=1, source_target_pairs={{0,4},{1,5},{2,6},{3,7},{8,12},{9,13},{10,14},{11,15},{16,20},{17,... | collective-permute-start | bytes 3145736 | tf_op jit(solution)/shard_map/ppermute | solution.py:20
  920.7 83.1 %collective-permute-start.7 = (f32[1,1,32,4,16,128]{5,4,3,2,1,0:T(8,128)S(1)}, f32[1,1,32,4,16,128]{5,4,3,2,1,0:T(8,128)S(1)}, u32[]{:S(2)}, u32[]{:S(2)}) collective-permute-start(f32[1,1,32,4,16,128]{5,4,3,2,1,0:T(8,128)S(1)} %bitcast.139), channel_id=1, source_target_pairs={{4,0},{5,1},{6,2},{7,3},{12,8},{13,9},{14,10},{15,11},{20,16},{21,... | collective-permute-start | bytes 3145736 | tf_op jit(solution)/shard_map/ppermute | solution.py:23
  1004.2 70.2 %collective-permute-start.8 = (f32[3,1,32,4,16,128]{5,4,3,2,1,0:T(8,128)S(1)}, f32[3,1,32,4,16,128]{5,4,3,2,1,0:T(8,128)S(1)}, u32[]{:S(2)}, u32[]{:S(2)}) collective-permute-start(f32[3,1,32,4,16,128]{5,4,3,2,1,0:T(8,128)S(1)} %pad_maximum_fusion), channel_id=1, source_target_pairs={{0,1},{1,2},{2,3},{4,5},{5,6},{6,7},{8,9},{9,10},{10,11},{12,13},{... | collective-permute-start | bytes 9437192 | tf_op jit(solution)/shard_map/ppermute | solution.py:20
  1007.6 70.9 %collective-permute-start.9 = (f32[3,1,32,4,16,128]{5,4,3,2,1,0:T(8,128)S(1)}, f32[3,1,32,4,16,128]{5,4,3,2,1,0:T(8,128)S(1)}, u32[]{:S(2)}, u32[]{:S(2)}) collective-permute-start(f32[3,1,32,4,16,128]{5,4,3,2,1,0:T(8,128)S(1)} %pad_maximum_fusion), channel_id=1, source_target_pairs={{1,0},{2,1},{3,2},{5,4},{6,5},{7,6},{9,8},{10,9},{11,10},{13,12},{... | collective-permute-start | bytes 9437192 | tf_op jit(solution)/shard_map/ppermute | solution.py:23
  (47 other events, 1174.6 us)
Sparse Core Ops, SparseCore 0:
  54.6 219.0 reduce-scatter.1
